TPU v7x, 32 devices: a whole 2x2x4 slice. The times are simulated.
32 devices in a mesh: fn: 32 (over z, y, x, core).
Axes of the slice: x: 2, y: 2, z: 4, core: 2. Of those that a mesh axis runs over, the one named last changes fastest.
Arguments:
- support_functions: float32 [96, 64, 2048], P('fn'), may hold values from -50 to 50
- owner_counts: int32 [32], replicated, may hold values from 1 to 3, as said below
- region_shift: int32 [96], P('fn'), may hold values from 0 to 63
- kernel: float32 [64, 64], replicated, may hold values from -0.75 to 0.75
- external: float32 [131072], P('fn'), may hold values from -1 to 1
- kinetic_taps: float32 [15], replicated, may hold values from -3 to 3
- magic_taps: float32 [16], replicated, may hold values from -0.6 to 1.6
Outputs:
- filtered: float32 [64, 64, 2048], P('fn')
Inputs may be any that keep to these rules, and one draw needn't show every extreme that they name: `owner_counts`: each owner's number of live slots; owners 2k and 2k+1 together hold exactly 4 live slots, so the counts sum to 64; slots at or past an owner's count hold no function.
All inputs are finite; a program needn't handle non-finite values.
Results may differ from a plain program's by a relative error of at most 0.0003.
Values sent between devices are 32-bit elements; how exact they have to be, the bound alone decides.
A program may use at most 64 MiB of HBM per device.

v0:
```python
import functools

import jax
import jax.numpy as jnp
from jax import lax
from jax.experimental import pallas as pl
from jax.experimental.pallas import tpu as pltpu
from jax.sharding import PartitionSpec as P

NY = 64
NZ = 32
LANES = 128
SLAB = 256
YS = SLAB // NZ
GROUP = 4
VMEM = pl.BlockSpec(memory_space=pltpu.VMEM)
SMEM = pl.BlockSpec(memory_space=pltpu.SMEM)
F32 = jnp.float32
BF16 = jnp.bfloat16


def halves(values):
    high = values.astype(BF16)
    low = (values - high.astype(F32)).astype(BF16)
    return high, low


def dot(left, right):
    return jnp.dot(left, right, preferred_element_type=F32)


def params(**more):
    return pltpu.CompilerParams(vmem_limit_bytes=48 << 20, has_side_effects="collective_id" in more, **more)


def roll_kernel(rows_per, shift_ref, slots_ref, own_ref, out_ref, flat_ref):
    slot_each, nx, cells = slots_ref.shape
    q_count = cells // LANES
    unit = min(rows_per, q_count)
    total = nx * q_count
    for s in range(slot_each):
        for q in range(q_count):
            flat_ref[s, pl.ds(q, nx, stride=q_count), :] = slots_ref[s, :, q * LANES:(q + 1) * LANES]
    for s in reversed(range(slot_each)):
        back = shift_ref[s] * q_count
        for u in range(total // unit):
            source = lax.rem(u * unit - back + total, total)
            block = flat_ref[s, pl.ds(pl.multiple_of(source, 8), unit), :]
            dest, within = u * unit // rows_per, u * unit % rows_per
            if s == slot_each - 1:
                out_ref[dest, within:within + unit, :] = block
            else:
                own_ref[dest, s * rows_per + within:s * rows_per + within + unit, :] = block


def matrices_kernel(devices, kin_ref, mag_ref, place_ref, kernel_ref, xf_ref, xb_ref, kin_out, fwd_out, bwd_out, mix_out):
    nx = xb_ref.shape[0]
    kin_half = kin_ref.shape[0]
    taps = mag_ref.shape[0]
    kin_count = 2 * kin_half - 1
    kin_center, mag_center = kin_count // 2, taps // 2
    kin = [-0.5 * kin_ref[abs(t - kin_center)] for t in range(kin_count)]
    mag = [mag_ref[t] for t in range(taps)]
    total = functools.reduce(lambda a, b: a + b, [jnp.abs(m) for m in mag])

    def picked(index, values, first=0):
        summed = jnp.zeros(index.shape, F32)
        for t, value in enumerate(values):
            summed = jnp.where(index == t + first, value, summed)
        return summed

    def iota(shape, dim):
        return lax.broadcasted_iota(jnp.int32, shape, dim)

    spread = max(nx // devices, 1)
    def x_of(row):
        if spread == 1:
            return row
        return lax.rem(row, devices) * spread + row // devices

    out_x, in_x = x_of(iota((nx, nx), 0)), x_of(iota((nx, nx), 1))
    ahead = lax.rem(in_x - out_x + mag_center + nx, nx)
    behind = lax.rem(out_x - in_x + mag_center + nx, nx)
    across = lax.rem(in_x - out_x + kin_center + nx, nx)
    fh, fl = halves(picked(ahead, mag) / total)
    kh, kl = halves(picked(across, kin))
    bh, bl = halves(picked(behind, mag) / total)
    xf_ref[:nx] = jnp.concatenate([fh, fl, fh], axis=1)
    xf_ref[nx:] = jnp.concatenate([kh, kl, kh], axis=1)
    xb_ref[...] = jnp.concatenate([bh, bl, bh], axis=1)

    square = (SLAB, SLAB)
    row, col = iota(square, 0), iota(square, 1)
    in_y, in_z = row // NZ, lax.rem(row, NZ)
    out_y, out_z = col // NZ, lax.rem(col, NZ)
    dy, dz = in_y - out_y, in_z - out_z

    def along_y(delta, values, center, d):
        low = max(YS * d + center - (YS - 1), 0)
        high = min(YS * d + center + YS - 1, len(values) - 1)
        return picked(delta + (YS * d + center), values[low:high + 1], low)

    mag_z = picked(lax.rem(dz + mag_center + NZ, NZ), mag) / total
    mag_zt = picked(lax.rem(mag_center - dz + NZ, NZ), mag) / total
    kin_z = picked(lax.rem(dz + kin_center + NZ, NZ), kin)
    reach = fwd_out.shape[0] // 2 // SLAB // 2
    kin_reach = kin_out.shape[0] // 2 // SLAB // 2
    for n in range(2 * reach + 1):
        d = n - reach
        for out, y_part, z_part in (
            (fwd_out, along_y(dy, mag, mag_center, d), mag_z),
            (bwd_out, along_y(-dy, mag, mag_center, -d), mag_zt),
        ):
            high, low = halves(y_part / total * z_part)
            out[n * SLAB:(n + 1) * SLAB] = high
            base = (2 * reach + 1 + n) * SLAB
            out[base:base + SLAB] = low
    for n in range(2 * kin_reach + 1):
        d = n - kin_reach
        value = jnp.where(dz == 0, along_y(dy, kin, kin_center, d), 0.0)
        if d == 0:
            value = value + jnp.where(dy == 0, kin_z, 0.0)
        high, low = halves(value)
        kin_out[n * SLAB:(n + 1) * SLAB] = high
        base = (2 * kin_reach + 1 + n) * SLAB
        kin_out[base:base + SLAB] = low

    functions = kernel_ref.shape[0]
    local = functions // devices
    full = (functions, functions)
    wanted = lax.rem(iota(full, 0), devices) * local + iota(full, 0) // devices
    row_pick = jnp.where(wanted == iota(full, 1), 1.0, 0.0).astype(BF16)
    col_pick = jnp.where(iota(full, 0) == place_ref[...], 1.0, 0.0).astype(BF16)
    parts = [dot(dot(row_pick, part).astype(BF16), col_pick).astype(BF16) for part in halves(kernel_ref[...])]
    mix_out[...] = jnp.concatenate([parts[0], parts[1], parts[0]], axis=1)


def partner(me, k):
    bit = 1
    there = me
    while bit <= k:
        if k & bit:
            there = there + bit - 2 * bit * ((me // bit) % 2)
        bit *= 2
    return there


def far_first(devices):
    half = devices // 2
    order = []
    for n in range(half):
        order += [half + n, n]
    return [k for k in order if k]


def greet(me, devices):
    barrier = pltpu.get_barrier_semaphore()
    for k in range(1, devices):
        pl.semaphore_signal(barrier, inc=1, device_id=(partner(me, k),), device_id_type=pl.DeviceIdType.MESH)
    pl.semaphore_wait(barrier, devices - 1)


def remote(source, target, send, recv, device):
    return pltpu.make_async_remote_copy(
        src_ref=source, dst_ref=target, send_sem=send, recv_sem=recv,
        device_id=(device,), device_id_type=pl.DeviceIdType.MESH,
    )


def scatter_kernel(devices, kin_ref, mag_ref, place_ref, kernel_ref, own_ref,
                   xf_ref, xb_ref, kin_out, fwd_out, bwd_out, mix_out, got_ref, send_sem, recv_sem):
    me = lax.axis_index("fn")
    greet(me, devices)
    copies = []
    for k in far_first(devices):
        there = partner(me, k)
        copy = remote(own_ref.at[there], got_ref.at[me], send_sem.at[k], recv_sem.at[k], there)
        copy.start()
        copies.append(copy)
    got_ref[me] = own_ref[me]
    matrices_kernel(devices, kin_ref, mag_ref, place_ref, kernel_ref, xf_ref, xb_ref, kin_out, fwd_out, bwd_out, mix_out)
    for copy in copies:
        copy.wait()


def return_kernel(devices, mixed_ref, pots_ref, got_ref, gpot_ref, send_sem, recv_sem, own_send, own_recv,
                  relay_send, relay_recv, core_send, core_recv):
    me = lax.axis_index("fn")
    half = devices // 2
    side = me // half
    across = partner(me, half)
    other_core = partner(me, 1)
    greet(me, devices)

    def to_core(source, owner, k):
        copy = remote(source, gpot_ref.at[owner], core_send.at[k], core_recv.at[k], other_core)
        copy.start()
        return copy

    handed = remote(pots_ref.at[1 - side], gpot_ref.at[me], own_send.at[0], own_recv.at[0], across)
    handed.start()
    direct, relays, blocks, core = {}, {}, [], []
    for k in range(2, half, 2):
        direct[k] = remote(pots_ref.at[side], gpot_ref.at[me], own_send.at[k], own_recv.at[k], partner(me, k))
        direct[k].start()
    core.append(to_core(pots_ref.at[side], me, 0))

    def give(ks):
        for k in ks:
            there = partner(me, k)
            copy = remote(mixed_ref.at[there], got_ref.at[me], send_sem.at[k], recv_sem.at[k], there)
            copy.start()
            blocks.append(copy)

    order = far_first(devices)
    ahead = len(order) // 3
    give(order[:ahead])
    handed.wait()
    for k in range(2, half, 2):
        relays[k] = remote(gpot_ref.at[across], gpot_ref.at[across], relay_send.at[k], relay_recv.at[k], partner(me, k))
        relays[k].start()
    core.append(to_core(gpot_ref.at[across], across, half))
    give(order[ahead:])
    got_ref[me] = mixed_ref[me]
    gpot_ref[me] = pots_ref[side]
    for k, copy in direct.items():
        copy.wait_recv()
        owner = partner(me, k)
        core.append(to_core(gpot_ref.at[owner], owner, k))
    for k, copy in relays.items():
        copy.wait_recv()
        owner = partner(me, k + half)
        core.append(to_core(gpot_ref.at[owner], owner, k + half))
    for copy in [*direct.values(), *relays.values()]:
        copy.wait_send()
    for copy in blocks + core:
        copy.wait()


def mix_kernel(devices, arrived_ref, mix_ref, external_ref, out_ref, pots_ref, up_ref, down_ref):
    functions = mix_ref.shape[0]
    local = functions // devices
    rows_per = external_ref.shape[0]
    stride = out_ref.shape[0] // devices
    half = devices // 2
    count = functions // 2
    for c in range(0, rows_per, 2):
        values = jnp.concatenate(
            [arrived_ref[pl.ds(c + k, functions, stride=rows_per), :] for k in range(2)], axis=1
        )
        high, low = halves(values)
        mixed = dot(mix_ref[...], jnp.concatenate([high, high, low], axis=0))
        up = down = 0.0
        for j in range(local):
            part = mixed[j * devices:(j + 1) * devices]
            for k in range(2):
                out_ref[pl.ds(j * rows_per + c + k, devices, stride=stride), :] = part[:, k * LANES:(k + 1) * LANES]
            squared = part * part
            up = up + jnp.sum(squared[:half], axis=0, keepdims=True)
            down = down + jnp.sum(squared[half:], axis=0, keepdims=True)
        for k in range(2):
            up_ref[c + k:c + k + 1, :] = up[:, k * LANES:(k + 1) * LANES]
            down_ref[c + k:c + k + 1, :] = down[:, k * LANES:(k + 1) * LANES]

    def cube_root(x):
        guess = jnp.exp(jnp.log(x) * (1.0 / 3.0))
        return guess - (guess - x / (guess * guess)) * (1.0 / 3.0)

    rho_up, rho_down = up_ref[...] / count, down_ref[...] / count
    shared = external_ref[...] + 0.5 * (rho_up + rho_down)
    spins = [shared - cube_root((6.0 / jnp.pi) * rho + 1e-6) for rho in (rho_up, rho_down)]
    peak = jnp.maximum(jnp.max(jnp.abs(spins[0])), jnp.max(jnp.abs(spins[1])))
    tail = jnp.full((8, LANES), peak, F32)
    for spin in range(2):
        pots_ref[spin, :rows_per] = spins[spin]
        pots_ref[spin, rows_per:] = tail


def filter_kernel(devices, rows_per, kin_ref, got_ref, gpot_ref, xf_ref, xb_ref, kinm_ref, fwd_ref, bwd_ref, out_ref,
                  v_hi, v_lo, p_hi, p_lo, w_hi, w_lo, acc_ref, pot_ref, stage_ref):
    local, nx, cells = out_ref.shape
    slabs = cells // SLAB
    q_count = cells // LANES
    per_slab = SLAB // LANES
    spread = max(rows_per // q_count, 1)

    def plane(field, q):
        ref, first = (gpot_ref, 0) if field == local else (got_ref, field * rows_per)
        stride = ref.shape[0] // devices
        if rows_per >= q_count:
            return jnp.concatenate([
                ref[pl.ds(first + xo * q_count + q, devices, stride=stride), :] for xo in range(spread)
            ], axis=0)
        split = q_count // rows_per
        start = (q // rows_per) * stride + first + q % rows_per
        return ref[pl.ds(start, nx, stride=split * stride), :]

    def slab_of(field, h):
        return jnp.concatenate([plane(field, h * per_slab + k) for k in range(per_slab)], axis=1)

    for h in range(slabs):
        pot_ref[h] = slab_of(local, h)
        for f in range(local):
            high, low = halves(slab_of(f, h))
            where = slice(f * nx, (f + 1) * nx)
            v_hi[h, where] = high
            v_lo[h, where] = low
            both = dot(xf_ref[...], jnp.concatenate([high, high, low], axis=0))
            p_hi[h, where], p_lo[h, where] = halves(both[:nx])
            acc_ref[h, where] = both[nx:]

    def banded(hi_ref, lo_ref, matrix_ref, h):
        width = matrix_ref.shape[0] // 2
        count = width // SLAB

        def wide(ref):
            return jnp.concatenate([
                jnp.concatenate(
                    [ref[lax.rem(h + g + (n - count // 2) + slabs, slabs)] for n in range(count)], axis=1
                ) for g in range(GROUP)
            ], axis=0)

        high, low = wide(hi_ref), wide(lo_ref)
        return dot(high, matrix_ref[:width]) + (dot(low, matrix_ref[:width]) + dot(high, matrix_ref[width:]))

    def forward(step, carry):
        h = step * GROUP
        kinetic = banded(v_hi, v_lo, kinm_ref, h)
        smooth = banded(p_hi, p_lo, fwd_ref, h)
        for g in range(GROUP):
            base = g * local * nx
            acc_ref[h + g] += kinetic[base:base + local * nx]
            potential = pot_ref[h + g]
            for f in range(local):
                high, low = halves(smooth[base + f * nx:base + (f + 1) * nx] * potential)
                mixed = dot(xb_ref[...], jnp.concatenate([high, high, low], axis=0))
                w_hi[h + g, f * nx:(f + 1) * nx], w_lo[h + g, f * nx:(f + 1) * nx] = halves(mixed)
        return carry

    lax.fori_loop(0, slabs // GROUP, forward, 0)

    sides = jnp.abs(kin_ref[0])
    for t in range(1, kin_ref.shape[0]):
        sides = sides + 2.0 * jnp.abs(kin_ref[t])
    peaks = gpot_ref[pl.ds(rows_per, devices, stride=gpot_ref.shape[0] // devices), :]
    bound = 1.0 + 1.5 * sides + jnp.max(peaks, axis=0, keepdims=True)
    bound = jnp.concatenate([bound] * per_slab, axis=1)

    def backward(step, carry):
        first = step * GROUP
        back = banded(w_hi, w_lo, bwd_ref, first)
        count = nx // spread
        for g in range(GROUP):
            h = first + g
            result = (acc_ref[h] + back[g * local * nx:(g + 1) * local * nx]) / bound
            for f in range(local):
                for k in range(per_slab):
                    q = h * per_slab + k
                    if spread > 1:
                        for xo in range(spread):
                            block = result[f * nx + xo * count:f * nx + (xo + 1) * count, k * LANES:(k + 1) * LANES]
                            stage_ref[f, q, pl.ds(xo, count, stride=spread), :] = block
                        ordered = stage_ref[f, q]
                    else:
                        ordered = result[f * nx:(f + 1) * nx, k * LANES:(k + 1) * LANES]
                    out_ref[f, :, pl.ds(pl.multiple_of(q * LANES, LANES), LANES)] = ordered
        return carry

    lax.fori_loop(0, slabs // GROUP, backward, 0)


def shaped(shape, dtype=F32):
    return jax.ShapeDtypeStruct(shape, dtype)


def body(support_functions, owner_counts, region_shift, kernel, external, kinetic_taps, magic_taps):
    devices = lax.axis_size("fn")
    position = lax.axis_index("fn")
    slot_each, nx, cells = support_functions.shape
    functions = kernel.shape[0]
    local = functions // devices
    rows_per = nx * cells // devices // LANES
    reach = -(-(magic_taps.shape[0] // 2) // YS)
    kin_reach = -(-(kinetic_taps.shape[0] - 1) // YS)

    own, outgoing = pl.pallas_call(
        functools.partial(roll_kernel, rows_per),
        out_shape=(shaped((devices, local * rows_per, LANES)), shaped((devices, rows_per, LANES))),
        in_specs=[SMEM, VMEM],
        out_specs=(VMEM, VMEM),
        scratch_shapes=[pltpu.VMEM((slot_each, nx * cells // LANES, LANES), F32)],
        compiler_params=params(),
        name="roll",
    )(region_shift, support_functions)

    route = [(d, d ^ 1) for d in range(devices)]
    received = lax.ppermute(outgoing, "fn", route)
    lone = owner_counts[position] < local
    balanced = own.at[:, rows_per:].set(jnp.where(lone, received, own[:, rows_per:]))

    pairs = jnp.arange(devices // 2, dtype=jnp.int32)[:, None] * (2 * local)
    counts = owner_counts.reshape(-1, 2)
    first = pairs + jnp.concatenate([jnp.zeros_like(counts[:, :1]), counts[:, :1]], axis=1)
    stand_in = pairs + jnp.asarray([[2 * local - 1, local]], jnp.int32)
    second = jnp.where(counts < local, stand_in, first + 1)
    places = jnp.stack([first, second], axis=-1).reshape(1, functions)

    each = pltpu.SemaphoreType.DMA((devices,))
    xf, xb, kin_m, fwd_m, bwd_m, mix_m, arrived = pl.pallas_call(
        functools.partial(scatter_kernel, devices),
        out_shape=(
            shaped((2 * nx, 3 * nx), BF16),
            shaped((nx, 3 * nx), BF16),
            shaped((2 * (2 * kin_reach + 1) * SLAB, SLAB), BF16),
            shaped((2 * (2 * reach + 1) * SLAB, SLAB), BF16),
            shaped((2 * (2 * reach + 1) * SLAB, SLAB), BF16),
            shaped((functions, 3 * functions), BF16),
            shaped((devices, local * rows_per, LANES)),
        ),
        in_specs=[SMEM, SMEM, VMEM, VMEM, VMEM],
        out_specs=(VMEM,) * 7,
        scratch_shapes=[each, each],
        compiler_params=params(collective_id=0),
        name="scatter",
    )(kinetic_taps, magic_taps, places, kernel, balanced)

    mixed, pots = pl.pallas_call(
        functools.partial(mix_kernel, devices),
        out_shape=(shaped((devices * local * rows_per, LANES)), shaped((2, rows_per + 8, LANES))),
        in_specs=[VMEM, VMEM, VMEM],
        out_specs=(VMEM, VMEM),
        scratch_shapes=[pltpu.VMEM((rows_per, LANES), F32)] * 2,
        compiler_params=params(),
        name="mix",
    )(arrived.reshape(-1, LANES), mix_m, external.reshape(rows_per, LANES))

    got, gpot = pl.pallas_call(
        functools.partial(return_kernel, devices),
        out_shape=(shaped((devices, local * rows_per, LANES)), shaped((devices, rows_per + 8, LANES))),
        in_specs=[VMEM, VMEM],
        out_specs=(VMEM, VMEM),
        scratch_shapes=[each] * 8,
        compiler_params=params(collective_id=1),
        name="give_back",
    )(mixed.reshape(devices, local * rows_per, LANES), pots)

    slabs = cells // SLAB
    tile = (slabs, local * nx, SLAB)
    return pl.pallas_call(
        functools.partial(filter_kernel, devices, rows_per),
        out_shape=shaped((local, nx, cells)),
        in_specs=[SMEM] + [VMEM] * 7,
        out_specs=VMEM,
        scratch_shapes=[pltpu.VMEM(tile, BF16)] * 6
        + [pltpu.VMEM(tile, F32), pltpu.VMEM((slabs, nx, SLAB), F32),
           pltpu.VMEM((local, cells // LANES, nx, LANES), F32)],
        compiler_params=params(),
        name="filter",
    )(kinetic_taps, got.reshape(-1, LANES), gpot.reshape(-1, LANES), xf, xb, kin_m, fwd_m, bwd_m)


def solution(mesh):
    placed = (P("fn", None, None), P(), P("fn"), P(), P("fn"), P(), P())
    return jax.shard_map(
        body, mesh=mesh, in_specs=placed, out_specs=P("fn", None, None), check_vma=False
    )
```

profile of v0, /device:TPU:0, one launch (start us, length us, event | category | flops | bytes accessed | tf_op | source)
XLA Modules:
  0.0 75.8 jit_solution(6734924137506342707)
XLA Ops:
  0.0 0.0 copy-start.6
  0.0 0.0 copy-start
  0.0 1.4 %copy-done = f32[3,64,2048]{2,1,0:T(8,128)S(1)} copy-done((f32[3,64,2048]{2,1,0:T(8,128)S(1)}, f32[3,64,2048]{2,1,0:T(8,128)}, u32[]{:S(2)}) %copy-start) | copy-done | bytes 1572888
  1.4 0.0 copy-start.4
  1.4 0.7 copy-done.4
  2.1 0.0 copy-start.7
  2.1 0.0 copy-start.1
  2.1 0.0 copy-start.3
  2.1 0.0 copy-start.5
  2.1 1.7 %roll.1 = (f32[32,64,128]{2,1,0:T(8,128)S(1)}, f32[32,32,128]{2,1,0:T(8,128)S(1)}) custom-call(s32[3]{0:T(128)S(1)} %copy-done.4, f32[3,64,2048]{2,1,0:T(8,128)S(1)} %copy-done), custom_call_target="tpu_custom_call" | custom-call | tf_op jit(solution)/shard_map/roll/pallas_call | solution.py:386
  3.8 0.0 copy-start.2
  3.8 0.5 collective-permute-start
  4.3 0.0 copy-done.7
  4.3 0.1 reshape.59
  4.4 0.6 dynamic_slice.3
  5.0 0.0 copy-done.6
  5.0 0.1 pad_add_fusion
  5.1 0.1 copy.12
  5.1 0.1 copy.13
  5.2 0.1 copy.14
  5.3 0.1 reshape.60.place_ref
  6.1 0.0 collective-permute-done
  6.1 0.1 select_dynamic-update-slice_fusion.own_ref
  6.3 0.0 copy-done.1
  6.3 0.0 copy-done.3
  6.3 0.0 copy-done.5
  6.3 26.3 %scatter.8 = (bf16[128,192]{1,0:T(8,128)(2,1)S(1)}, bf16[64,192]{1,0:T(8,128)(2,1)S(1)}, bf16[2560,256]{1,0:T(8,128)(2,1)S(1)}, bf16[1536,256]{1,0:T(8,128)(2,1)...) custom-call(f32[15]{0:T(128)S(1)} %copy-done.3, f32[16]{0:T(128)S(1)} %copy-done.5, ...), custom_call_target="tpu_custom_call" | custom-call | tf_op jit(solution)/shard_map/scatter/pallas_call | solution.py:409
  32.6 0.0 copy-done.2
  32.6 1.5 %mix.1 = (f32[2048,128]{1,0:T(8,128)S(1)}, f32[2,40,128]{2,1,0:T(8,128)S(1)}) custom-call(f32[2048,128]{1,0:T(8,128)S(1)} %bitcast.9, bf16[64,192]{1,0:T(8,128)(2,1)S(1)} %get-tuple-element.33.mix_ref, f32[32,128]{1,0:T(8,128)S(1)} %bitcast.13), custom_call_target="tpu_custom_call" | custom-call | tf_op jit(solution)/shard_map/mix/pallas_call | solution.py:427
  34.1 33.6 %give_back.1 = (f32[32,64,128]{2,1,0:T(8,128)S(1)}, f32[32,40,128]{2,1,0:T(8,128)S(1)}) custom-call(f32[32,64,128]{2,1,0:T(8,128)S(1)} %bitcast.10, f32[2,40,128]{2,1,0:T(8,128)S(1)} %get-tuple-element.35.pots_ref), custom_call_target="tpu_custom_call" | custom-call | tf_op jit(solution)/shard_map/give_back/pallas_call | solution.py:437
  67.7 8.1 %filter.1 = f32[2,64,2048]{2,1,0:T(8,128)} custom-call(f32[15]{0:T(128)S(1)} %copy-done.3, f32[2048,128]{1,0:T(8,128)S(1)} %bitcast.11, f32[1280,128]{1,0:T(8,128)S(1)} %bitcast.12, bf16[128,192]{1,0:T(8,128)(2,1)S(1)} %get-tuple-element.38.xf_ref, bf16[64,192]{1,0:T(8,128)(2,1)S(1)} %get-tuple-element.39.xb_ref, ...), custom_call_target="tpu_custom_call" | custom-call | tf_op jit(solution)/shard_map/filter/pallas_call | solution.py:449
  (2 shorter events, 0.0 us)
Async XLA Ops:
  0.0 5.0 %copy-start.6 = (s32[2]{0:T(128)S(1)}, s32[2]{0:T(128)}, u32[]{:S(2)}) copy-start(s32[2]{0:T(128)} %constant.52) | copy-start | bytes 28
  0.0 1.4 %copy-start = (f32[3,64,2048]{2,1,0:T(8,128)S(1)}, f32[3,64,2048]{2,1,0:T(8,128)}, u32[]{:S(2)}) copy-start(f32[3,64,2048]{2,1,0:T(8,128)} %slots_ref.1) | copy-start | bytes 4718596
  1.4 0.7 copy-start.4
  2.1 2.2 %copy-start.7 = (s32[32]{0:T(128)S(1)}, s32[32]{0:T(128)}, u32[]{:S(2)}) copy-start(s32[32]{0:T(128)} %param.11) | copy-start | bytes 388
  2.1 4.2 %copy-start.1 = (f32[64,64]{1,0:T(8,128)S(1)}, f32[64,64]{1,0:T(8,128)}, u32[]{:S(2)}) copy-start(f32[64,64]{1,0:T(8,128)} %kernel_ref.1) | copy-start | bytes 49156
  2.1 4.2 %copy-start.3 = (f32[15]{0:T(128)S(1)}, f32[15]{0:T(128)}, u32[]{:S(2)}) copy-start(f32[15]{0:T(128)} %kin_ref.3) | copy-start | bytes 184
  2.1 4.2 %copy-start.5 = (f32[16]{0:T(128)S(1)}, f32[16]{0:T(128)}, u32[]{:S(2)}) copy-start(f32[16]{0:T(128)} %mag_ref.1) | copy-start | bytes 196
  3.8 28.8 %copy-start.2 = (f32[4096]{0:T(1024)S(1)}, f32[4096]{0:T(1024)}, u32[]{:S(2)}) copy-start(f32[4096]{0:T(1024)} %param.14) | copy-start | bytes 49156
  3.8 2.3 %collective-permute-start = (f32[32,32,128]{2,1,0:T(8,128)S(1)}, f32[32,32,128]{2,1,0:T(8,128)S(1)}, u32[]{:S(2)}, u32[]{:S(2)}) collective-permute-start(f32[32,32,128]{2,1,0:T(8,128)S(1)} %get-tuple-element.31), channel_id=1, source_target_pairs={{0,1},{1,0},{2,3},{3,2},{4,5},{5,4},{6,7},{7,6},{8,9},{9,8},{10,11... | collective-permute-start | bytes 1572872 | tf_op jit(solution)/shard_map/ppermute | solution.py:397
where the time goes:
time: 76.6 us; the launch traced here: 75.8 us
  Pallas kernels  71.2 us (93%)
  local copies, waits for them, and re-layouts  3.15 us (4%)
    pallas_call x1, Pallas kernels, body(): pl.pallas_call(functools.partial(return_kernel, devices), out_shape=(shap...  33.6 us
    pallas_call x1, Pallas kernels, body(): pl.pallas_call(functools.partial(scatter_kernel, devices), out_shape=(sha...  26.3 us
    pallas_call x1, Pallas kernels, body(): pl.pallas_call(functools.partial(filter_kernel, devices, rows_per), out_s...  8.12 us
    unnamed x16, local copies, waits for them, and re-layouts  2.1 us
    pallas_call x1, Pallas kernels, body(): pl.pallas_call(functools.partial(roll_kernel, rows_per), out_shape=(shape...  1.67 us
  transfers between devices with their start and end apart: 1, of which 0 were waited for; matrix products, arithmetic and copies ran while one was open for 1% of the time, Pallas kernels for 0%

commit v1 on v0

v1 whole, which is shorter than its diff:
```python
import functools

import jax
import jax.numpy as jnp
from jax import lax
from jax.experimental import pallas as pl
from jax.experimental.pallas import tpu as pltpu
from jax.sharding import PartitionSpec as P

NY = 64
NZ = 32
LANES = 128
SLAB = 256
YS = SLAB // NZ
GROUP = 4
VMEM = pl.BlockSpec(memory_space=pltpu.VMEM)
SMEM = pl.BlockSpec(memory_space=pltpu.SMEM)
HBM = pl.BlockSpec(memory_space=pltpu.HBM)
F32 = jnp.float32
BF16 = jnp.bfloat16


def halves(values):
    high = values.astype(BF16)
    low = (values - high.astype(F32)).astype(BF16)
    return high, low


def dot(left, right):
    return jnp.dot(left, right, preferred_element_type=F32)


def params(**more):
    return pltpu.CompilerParams(vmem_limit_bytes=48 << 20, has_side_effects="collective_id" in more, **more)


def x_of(row, devices, spread):
    if spread == 1:
        return row
    return lax.rem(row, devices) * spread + row // devices


def matrices(devices, kin_ref, mag_ref, xf_ref, xb_ref, kin_out, fwd_out, bwd_out):
    nx = xb_ref.shape[0]
    kin_half = kin_ref.shape[0]
    taps = mag_ref.shape[0]
    kin_count = 2 * kin_half - 1
    kin_center, mag_center = kin_count // 2, taps // 2
    kin = [-0.5 * kin_ref[abs(t - kin_center)] for t in range(kin_count)]
    mag = [mag_ref[t] for t in range(taps)]
    total = functools.reduce(lambda a, b: a + b, [jnp.abs(m) for m in mag])

    def picked(index, values, first=0):
        summed = jnp.zeros(index.shape, F32)
        for t, value in enumerate(values):
            summed = jnp.where(index == t + first, value, summed)
        return summed

    def iota(shape, dim):
        return lax.broadcasted_iota(jnp.int32, shape, dim)

    spread = max(nx // devices, 1)
    out_x, in_x = (x_of(iota((nx, nx), d), devices, spread) for d in (0, 1))
    ahead = lax.rem(in_x - out_x + mag_center + nx, nx)
    behind = lax.rem(out_x - in_x + mag_center + nx, nx)
    across = lax.rem(in_x - out_x + kin_center + nx, nx)
    fh, fl = halves(picked(ahead, mag) / total)
    kh, kl = halves(picked(across, kin))
    bh, bl = halves(picked(behind, mag) / total)
    xf_ref[:nx] = jnp.concatenate([fh, fl, fh], axis=1)
    xf_ref[nx:] = jnp.concatenate([kh, kl, kh], axis=1)
    xb_ref[...] = jnp.concatenate([bh, bl, bh], axis=1)

    square = (SLAB, SLAB)
    row, col = iota(square, 0), iota(square, 1)
    in_y, in_z = row // NZ, lax.rem(row, NZ)
    out_y, out_z = col // NZ, lax.rem(col, NZ)
    dy, dz = in_y - out_y, in_z - out_z

    def along_y(delta, values, center, d):
        low = max(YS * d + center - (YS - 1), 0)
        high = min(YS * d + center + YS - 1, len(values) - 1)
        return picked(delta + (YS * d + center), values[low:high + 1], low)

    mag_z = picked(lax.rem(dz + mag_center + NZ, NZ), mag) / total
    mag_zt = picked(lax.rem(mag_center - dz + NZ, NZ), mag) / total
    kin_z = picked(lax.rem(dz + kin_center + NZ, NZ), kin)
    reach = fwd_out.shape[0] // 2 // SLAB // 2
    kin_reach = kin_out.shape[0] // 2 // SLAB // 2
    for n in range(2 * reach + 1):
        d = n - reach
        for out, y_part, z_part in (
            (fwd_out, along_y(dy, mag, mag_center, d), mag_z),
            (bwd_out, along_y(-dy, mag, mag_center, -d), mag_zt),
        ):
            high, low = halves(y_part / total * z_part)
            out[n * SLAB:(n + 1) * SLAB] = high
            base = (2 * reach + 1 + n) * SLAB
            out[base:base + SLAB] = low
    for n in range(2 * kin_reach + 1):
        d = n - kin_reach
        value = jnp.where(dz == 0, along_y(dy, kin, kin_center, d), 0.0)
        if d == 0:
            value = value + jnp.where(dy == 0, kin_z, 0.0)
        high, low = halves(value)
        kin_out[n * SLAB:(n + 1) * SLAB] = high
        base = (2 * kin_reach + 1 + n) * SLAB
        kin_out[base:base + SLAB] = low


def mixing_matrix(devices, counts_ref, kernel_ref, mix_out):
    functions = kernel_ref.shape[0]
    local = functions // devices
    full = (functions, functions)
    row, col = (lax.broadcasted_iota(jnp.int32, full, d) for d in (0, 1))
    lead = jnp.zeros((1, functions), jnp.int32)
    lane = lax.broadcasted_iota(jnp.int32, (1, functions), 1)
    pair = lane // (2 * local)
    for k in range(devices // 2):
        lead = jnp.where(pair == k, counts_ref[2 * k], lead)
    slot = lax.rem(lane, local)
    odd = lax.rem(lane // local, 2) == 1
    count = jnp.where(odd, 2 * local - lead, lead)
    first = jnp.where(odd, lead, 0)
    stand_in = jnp.where(odd, local, 2 * local - 1)
    second = jnp.where(count < local, stand_in, first + 1)
    place = pair * (2 * local) + jnp.where(slot == 0, first, second)
    wanted = lax.rem(row, devices) * local + row // devices
    row_pick = jnp.where(wanted == col, 1.0, 0.0).astype(BF16)
    col_pick = jnp.where(row == place, 1.0, 0.0).astype(BF16)
    parts = [dot(dot(row_pick, part).astype(BF16), col_pick).astype(BF16) for part in halves(kernel_ref[...])]
    mix_out[...] = jnp.concatenate([parts[0], parts[1], parts[0]], axis=1)


def partner(me, k):
    bit = 1
    there = me
    while bit <= k:
        if k & bit:
            there = there + bit - 2 * bit * ((me // bit) % 2)
        bit *= 2
    return there


def far_first(devices):
    half = devices // 2
    order = []
    for n in range(half):
        order += [half + n, n]
    return [k for k in order if k]


def remote(source, target, send, recv, device):
    return pltpu.make_async_remote_copy(
        src_ref=source, dst_ref=target, send_sem=send, recv_sem=recv,
        device_id=(device,), device_id_type=pl.DeviceIdType.MESH,
    )


def cube_root(x):
    guess = jnp.exp(jnp.log(x) * (1.0 / 3.0))
    return guess - (guess - x / (guess * guess)) * (1.0 / 3.0)


def exchange_kernel(devices, parts,
                    slots_hbm, shift_hbm, counts_hbm, kernel_hbm, external_hbm, kin_hbm, mag_hbm,
                    xf_ref, xb_ref, kin_out, fwd_out, bwd_out, back_ref, gpot_ref,
                    raw_ref, own_ref, out_ref, in_ref, got_ref, mixed_ref, pots_ref,
                    mix_ref, kernel_ref, external_ref, up_ref, down_ref,
                    shift_ref, counts_ref, kin_ref, mag_ref,
                    load_sem, swap_sem, lead_send, lead_recv, part_send, part_recv,
                    back_send, back_recv, pot_send, pot_recv):
    slot_each, nx, cells = raw_ref.shape
    functions = kernel_ref.shape[0]
    local = functions // devices
    q_count = cells // LANES
    rows_per = external_ref.shape[0]
    rows = rows_per // parts
    half = devices // 2
    count = functions // 2
    me = lax.axis_index("fn")
    side = me // half
    across = partner(me, half)
    mate = partner(me, 1)

    def load(source, target, k):
        copy = pltpu.make_async_copy(source, target, load_sem.at[k])
        copy.start()
        return copy

    slot_loads = {0: load(slots_hbm.at[0], raw_ref.at[0], 0)}
    shift_load = load(shift_hbm, shift_ref, slot_each)
    for s in reversed(range(1, slot_each)):
        slot_loads[s] = load(slots_hbm.at[s], raw_ref.at[s], s)
    small = [load(a, b, slot_each + 1 + k) for k, (a, b) in enumerate((
        (counts_hbm, counts_ref), (kernel_hbm, kernel_ref), (external_hbm, external_ref),
        (kin_hbm, kin_ref), (mag_hbm, mag_ref),
    ))]

    barrier = pltpu.get_barrier_semaphore()
    for k in range(1, devices):
        pl.semaphore_signal(barrier, inc=1, device_id=(partner(me, k),), device_id_type=pl.DeviceIdType.MESH)
    order = far_first(devices)

    def block(part, device, field=0):
        return pl.multiple_of(((part * devices + device) * local + field) * rows, 8)

    spread = max(rows_per // q_count, 1)
    x_row = lax.broadcasted_iota(jnp.int32, (nx, nx), 0)
    x_col = lax.broadcasted_iota(jnp.int32, (nx, nx), 1)
    x_row = x_of(x_row, devices, spread)

    def rolled(s, target, fields, field):
        picked = lax.rem(x_row - shift_ref[s] + nx, nx) == x_col
        pick = jnp.where(picked, 1.0, 0.0).astype(BF16)
        pick = jnp.concatenate([pick, pick], axis=1)
        slot_loads[s].wait()
        for h in range(cells // SLAB):
            high, low = halves(raw_ref[s, :, h * SLAB:(h + 1) * SLAB])
            moved = dot(pick, jnp.concatenate([high, low], axis=0))
            for k in range(SLAB // LANES):
                q = h * (SLAB // LANES) + k
                column = moved[:, k * LANES:(k + 1) * LANES]
                if rows_per >= q_count:
                    for xo in range(spread):
                        at = xo * q_count + q
                        start = (at // rows * devices * fields + field) * rows + at % rows
                        target[pl.ds(start, devices, stride=fields * rows), :] = (
                            column[xo * devices:(xo + 1) * devices]
                        )
                else:
                    start = (q // rows * fields + field) * rows + q % rows
                    target[pl.ds(start, nx, stride=q_count // rows * fields * rows), :] = column

    shift_load.wait()
    rolled(0, own_ref, local, 0)
    pl.semaphore_wait(barrier, devices - 1)

    sends = []
    arrivals = [[] for _ in range(parts)]

    def give(part, first, fields, k, send, recv):
        there = partner(me, k)
        copy = remote(own_ref.at[pl.ds(block(part, there, first), fields * rows)],
                      got_ref.at[pl.ds(block(part, me, first), fields * rows)], send.at[k], recv.at[k], there)
        copy.start()
        sends.append(copy)
        arrivals[part].append(copy)

    for k in order:
        give(0, 0, 1, k, lead_send, lead_recv)
    last = slot_each - 1
    rolled(last, out_ref, 1, 0)
    swap = remote(out_ref, in_ref, swap_sem.at[0], swap_sem.at[1], mate)
    swap.start()
    rolled(1, own_ref, local, 1)
    for copy in small:
        copy.wait()
    swap.wait_recv()
    lone = jnp.full((rows, LANES), counts_ref[me], jnp.int32) < local
    for part in range(parts):
        for dest in range(devices):
            where = ((part * devices + dest) * local + 1) * rows
            there = (part * devices + dest) * rows
            mine = own_ref[where:where + rows, :]
            own_ref[where:where + rows, :] = jnp.where(lone, in_ref[there:there + rows, :], mine)
    for k in order:
        give(0, 1, local - 1, k, part_send.at[0], part_recv.at[0])
    for part in range(1, parts):
        for k in order:
            give(part, 0, local, k, part_send.at[part], part_recv.at[part])
    for part in range(parts):
        got_ref[pl.ds(block(part, me), local * rows), :] = own_ref[pl.ds(block(part, me), local * rows), :]

    mixing_matrix(devices, counts_ref, kernel_ref, mix_ref)
    matrices(devices, kin_ref, mag_ref, xf_ref, xb_ref, kin_out, fwd_out, bwd_out)

    def mix(part):
        base = part * functions * rows
        for c in range(0, rows, 2):
            values = jnp.concatenate(
                [got_ref[pl.ds(base + c + k, functions, stride=rows), :] for k in range(2)], axis=1
            )
            high, low = halves(values)
            mixed = dot(mix_ref[...], jnp.concatenate([high, high, low], axis=0))
            up = down = 0.0
            for j in range(local):
                piece = mixed[j * devices:(j + 1) * devices]
                for k in range(2):
                    mixed_ref[pl.ds(base + j * rows + c + k, devices, stride=local * rows), :] = (
                        piece[:, k * LANES:(k + 1) * LANES]
                    )
                squared = piece * piece
                up = up + jnp.sum(squared[:half], axis=0, keepdims=True)
                down = down + jnp.sum(squared[half:], axis=0, keepdims=True)
            for k in range(2):
                up_ref[c + k:c + k + 1, :] = up[:, k * LANES:(k + 1) * LANES]
                down_ref[c + k:c + k + 1, :] = down[:, k * LANES:(k + 1) * LANES]
        rho_up, rho_down = up_ref[...] / count, down_ref[...] / count
        shared = external_ref[part * rows:(part + 1) * rows, :] + 0.5 * (rho_up + rho_down)
        spins = [shared - cube_root((6.0 / jnp.pi) * rho + 1e-6) for rho in (rho_up, rho_down)]
        for spin in range(2):
            pots_ref[spin, part * rows:(part + 1) * rows] = spins[spin]
        sizes = jnp.maximum(jnp.abs(spins[0]), jnp.abs(spins[1]))
        peak = sizes[:8]
        for w in range(1, rows // 8):
            peak = jnp.maximum(peak, sizes[w * 8:(w + 1) * 8])
        return peak

    peak = None
    returns, handed, waits = [], [], []
    for part in range(parts):
        for copy in arrivals[part]:
            copy.wait_recv()
        here = mix(part)
        peak = here if peak is None else jnp.maximum(peak, here)
        begin, extent = part * rows, rows
        if part == parts - 1:
            extent = rows + 8
            for spin in range(2):
                pots_ref[spin, rows_per:] = peak
        span = pl.ds(begin, extent)

        def show(source, owner, slot, there):
            copy = remote(source, gpot_ref.at[owner, span], pot_send.at[part, slot], pot_recv.at[part, slot], there)
            copy.start()
            return copy

        handed = show(pots_ref.at[1 - side, span], me, 0, across)
        sends.append(handed)
        for k in range(1, half):
            waits.append(show(pots_ref.at[side, span], me, k, partner(me, k)))
        for k in order:
            there = partner(me, k)
            copy = remote(mixed_ref.at[pl.ds(block(part, there), local * rows)],
                          back_ref.at[pl.ds(block(part, me), local * rows)],
                          back_send.at[part, k], back_recv.at[part, k], there)
            copy.start()
            returns.append(copy)
        back_ref[pl.ds(block(part, me), local * rows), :] = mixed_ref[pl.ds(block(part, me), local * rows), :]
        gpot_ref[me, begin:begin + extent] = pots_ref[side, begin:begin + extent]
        handed.wait_recv()
        for k in range(1, half):
            waits.append(show(gpot_ref.at[across, span], across, half + k, partner(me, k)))
    for copy in returns + waits:
        copy.wait_recv()
    for copy in [swap, *sends, *returns, *waits]:
        copy.wait_send()


def filter_kernel(devices, rows_per, parts, kin_ref, got_ref, gpot_ref, xf_ref, xb_ref, kinm_ref, fwd_ref, bwd_ref, out_ref,
                  v_hi, v_lo, p_hi, p_lo, w_hi, w_lo, acc_ref, pot_ref, stage_ref):
    local, nx, cells = out_ref.shape
    slabs = cells // SLAB
    q_count = cells // LANES
    per_slab = SLAB // LANES
    spread = max(rows_per // q_count, 1)

    rows = rows_per // parts
    pot_rows = gpot_ref.shape[0] // devices

    def plane(field, q):
        if field == local:
            ref, stride, extent = gpot_ref, pot_rows, rows_per
        else:
            ref, stride, extent = got_ref, local * rows, rows

        def start(x):
            if field == local:
                return x
            return (x // rows * devices * local + field) * rows + x % rows

        if rows_per >= q_count:
            return jnp.concatenate([
                ref[pl.ds(start(xo * q_count + q), devices, stride=stride), :] for xo in range(spread)
            ], axis=0)
        split = q_count // extent
        return ref[pl.ds((q // extent) * stride + start(q % extent), nx, stride=split * stride), :]

    def slab_of(field, h):
        return jnp.concatenate([plane(field, h * per_slab + k) for k in range(per_slab)], axis=1)

    for h in range(slabs):
        pot_ref[h] = slab_of(local, h)
        for f in range(local):
            high, low = halves(slab_of(f, h))
            where = slice(f * nx, (f + 1) * nx)
            v_hi[h, where] = high
            v_lo[h, where] = low
            both = dot(xf_ref[...], jnp.concatenate([high, high, low], axis=0))
            p_hi[h, where], p_lo[h, where] = halves(both[:nx])
            acc_ref[h, where] = both[nx:]

    def banded(hi_ref, lo_ref, matrix_ref, h):
        width = matrix_ref.shape[0] // 2
        count = width // SLAB

        def wide(ref):
            return jnp.concatenate([
                jnp.concatenate(
                    [ref[lax.rem(h + g + (n - count // 2) + slabs, slabs)] for n in range(count)], axis=1
                ) for g in range(GROUP)
            ], axis=0)

        high, low = wide(hi_ref), wide(lo_ref)
        return dot(high, matrix_ref[:width]) + (dot(low, matrix_ref[:width]) + dot(high, matrix_ref[width:]))

    def forward(step, carry):
        h = step * GROUP
        kinetic = banded(v_hi, v_lo, kinm_ref, h)
        smooth = banded(p_hi, p_lo, fwd_ref, h)
        for g in range(GROUP):
            base = g * local * nx
            acc_ref[h + g] += kinetic[base:base + local * nx]
            potential = pot_ref[h + g]
            for f in range(local):
                high, low = halves(smooth[base + f * nx:base + (f + 1) * nx] * potential)
                mixed = dot(xb_ref[...], jnp.concatenate([high, high, low], axis=0))
                w_hi[h + g, f * nx:(f + 1) * nx], w_lo[h + g, f * nx:(f + 1) * nx] = halves(mixed)
        return carry

    lax.fori_loop(0, slabs // GROUP, forward, 0)

    sides = jnp.abs(kin_ref[0])
    for t in range(1, kin_ref.shape[0]):
        sides = sides + 2.0 * jnp.abs(kin_ref[t])
    peaks = gpot_ref[rows_per:pot_rows, :]
    for e in range(1, devices):
        peaks = jnp.maximum(peaks, gpot_ref[e * pot_rows + rows_per:(e + 1) * pot_rows, :])
    bound = 1.0 + 1.5 * sides + jnp.max(peaks)

    def backward(step, carry):
        first = step * GROUP
        back = banded(w_hi, w_lo, bwd_ref, first)
        count = nx // spread
        for g in range(GROUP):
            h = first + g
            result = (acc_ref[h] + back[g * local * nx:(g + 1) * local * nx]) / bound
            for f in range(local):
                for k in range(per_slab):
                    q = h * per_slab + k
                    if spread > 1:
                        for xo in range(spread):
                            block = result[f * nx + xo * count:f * nx + (xo + 1) * count, k * LANES:(k + 1) * LANES]
                            stage_ref[f, q, pl.ds(xo, count, stride=spread), :] = block
                        ordered = stage_ref[f, q]
                    else:
                        ordered = result[f * nx:(f + 1) * nx, k * LANES:(k + 1) * LANES]
                    out_ref[f, :, pl.ds(pl.multiple_of(q * LANES, LANES), LANES)] = ordered
        return carry

    lax.fori_loop(0, slabs // GROUP, backward, 0)


def shaped(shape, dtype=F32):
    return jax.ShapeDtypeStruct(shape, dtype)


def body(support_functions, owner_counts, region_shift, kernel, external, kinetic_taps, magic_taps):
    devices = lax.axis_size("fn")
    slot_each, nx, cells = support_functions.shape
    functions = kernel.shape[0]
    local = functions // devices
    rows_per = nx * cells // devices // LANES
    q_count = cells // LANES
    parts = 2 if rows_per % (2 * q_count) == 0 else 1
    rows = rows_per // parts
    reach = -(-(magic_taps.shape[0] // 2) // YS)
    kin_reach = -(-(kinetic_taps.shape[0] - 1) // YS)

    each = pltpu.SemaphoreType.DMA((devices,))
    each_part = pltpu.SemaphoreType.DMA((parts, devices))
    flat = (nx * q_count, LANES)
    whole = (functions * rows_per, LANES)
    xf, xb, kin_m, fwd_m, bwd_m, back, gpot = pl.pallas_call(
        functools.partial(exchange_kernel, devices, parts),
        out_shape=(
            shaped((2 * nx, 3 * nx), BF16),
            shaped((nx, 3 * nx), BF16),
            shaped((2 * (2 * kin_reach + 1) * SLAB, SLAB), BF16),
            shaped((2 * (2 * reach + 1) * SLAB, SLAB), BF16),
            shaped((2 * (2 * reach + 1) * SLAB, SLAB), BF16),
            shaped(whole),
            shaped((devices, rows_per + 8, LANES)),
        ),
        in_specs=[HBM] * 7,
        out_specs=(VMEM,) * 7,
        scratch_shapes=[
            pltpu.VMEM((slot_each, nx, cells), F32), pltpu.VMEM(whole, F32),
            pltpu.VMEM(flat, F32), pltpu.VMEM(flat, F32), pltpu.VMEM(whole, F32), pltpu.VMEM(whole, F32),
            pltpu.VMEM((2, rows_per + 8, LANES), F32), pltpu.VMEM((functions, 3 * functions), BF16),
            pltpu.VMEM((functions, functions), F32), pltpu.VMEM((rows_per, LANES), F32),
            pltpu.VMEM((rows, LANES), F32), pltpu.VMEM((rows, LANES), F32),
            pltpu.SMEM(region_shift.shape, jnp.int32), pltpu.SMEM(owner_counts.shape, jnp.int32),
            pltpu.SMEM(kinetic_taps.shape, F32), pltpu.SMEM(magic_taps.shape, F32),
            pltpu.SemaphoreType.DMA((slot_each + 6,)), pltpu.SemaphoreType.DMA((2,)), each, each,
        ] + [each_part] * 6,
        compiler_params=params(collective_id=0),
        name="exchange",
    )(support_functions, region_shift, owner_counts, kernel, external.reshape(rows_per, LANES), kinetic_taps, magic_taps)

    slabs = cells // SLAB
    tile = (slabs, local * nx, SLAB)
    return pl.pallas_call(
        functools.partial(filter_kernel, devices, rows_per, parts),
        out_shape=shaped((local, nx, cells)),
        in_specs=[SMEM] + [VMEM] * 7,
        out_specs=VMEM,
        scratch_shapes=[pltpu.VMEM(tile, BF16)] * 6
        + [pltpu.VMEM(tile, F32), pltpu.VMEM((slabs, nx, SLAB), F32),
           pltpu.VMEM((local, cells // LANES, nx, LANES), F32)],
        compiler_params=params(),
        name="filter",
    )(kinetic_taps, back, gpot.reshape(-1, LANES), xf, xb, kin_m, fwd_m, bwd_m)


def solution(mesh):
    placed = (P("fn", None, None), P(), P("fn"), P(), P("fn"), P(), P())
    return jax.shard_map(
        body, mesh=mesh, in_specs=placed, out_specs=P("fn", None, None), check_vma=False
    )
```

time: 76.6 us -> 70.7 us (0.923)
  Pallas kernels: 71.2 us -> 66.3 us
  local copies, waits for them, and re-layouts: 3.15 us -> 4.09 us
    pallas_call x5 -> x2, Pallas kernels: 71.2 us -> 66.3 us  [the longest x1 58.1 us: body(): pl.pallas_call(functools.partial(exchange_kernel, devices, parts), out_sh...]
    unnamed x16 -> x12, local copies, waits for them, and re-layouts: 2.1 us -> 4.09 us
  transfers between devices with their start and end apart: 1 -> 0, of which waited for: 0 -> 0; matrix products, arithmetic and copies ran while one was open for 1% -> 0% of each run, Pallas kernels for 0% -> 0%
where the time goes in v1:
time: 70.7 us; the launch traced here: 70.4 us
  Pallas kernels  66.3 us (94%)
  local copies, waits for them, and re-layouts  4.09 us (6%)
    pallas_call x1, Pallas kernels, body(): pl.pallas_call(functools.partial(exchange_kernel, devices, parts), out_sh...  58.1 us
    pallas_call x1, Pallas kernels, body(): pl.pallas_call(functools.partial(filter_kernel, devices, rows_per, parts)...  8.13 us
    unnamed x12, local copies, waits for them, and re-layouts  4.09 us

profile of v1, /device:TPU:0, one launch (start us, length us, event | category | flops | bytes accessed | tf_op | source)
XLA Modules:
  0.0 70.4 jit_solution(17266919951521804851)
XLA Ops:
  0.0 0.0 copy-start
  0.0 0.8 %copy-done = f32[64,64]{1,0:T(8,128)S(1)} copy-done((f32[64,64]{1,0:T(8,128)S(1)}, f32[64,64]{1,0:T(8,128)}, u32[]{:S(2)}) %copy-start) | copy-done | bytes 16408
  0.8 0.0 copy-start.1
  0.8 0.7 %copy-done.1 = f32[4096]{0:T(1024)S(1)} copy-done((f32[4096]{0:T(1024)S(1)}, f32[4096]{0:T(1024)}, u32[]{:S(2)}) %copy-start.1) | copy-done | bytes 16408
  1.5 0.0 copy-start.2
  1.5 0.7 copy-done.2
  2.1 0.0 copy-start.3
  2.1 0.7 copy-done.3
  2.8 0.0 copy-start.4
  2.8 0.7 copy-done.4
  3.4 0.0 copy-start.5
  3.4 0.7 copy-done.5
  4.1 58.1 %exchange.1 = (bf16[128,192]{1,0:T(8,128)(2,1)S(1)}, bf16[64,192]{1,0:T(8,128)(2,1)S(1)}, bf16[2560,256]{1,0:T(8,128)(2,1)S(1)}, bf16[1536,256]{1,0:T(8,128)(2,1...) custom-call(f32[3,64,2048]{2,1,0:T(8,128)} %slots_hbm.1, ...), custom_call_target="tpu_custom_call" | custom-call | tf_op jit(solution)/shard_map/exchange/pallas_call | solution.py:475
  62.3 8.1 %filter.1 = f32[2,64,2048]{2,1,0:T(8,128)} custom-call(f32[15]{0:T(128)S(1)} %copy-done.2, f32[2048,128]{1,0:T(8,128)S(1)} %get-tuple-element.12.got_ref, f32[1280,128]{1,0:T(8,128)S(1)} %bitcast.2, bf16[128,192]{1,0:T(8,128)(2,1)S(1)} %get-tuple-element.14.xf_ref, bf16[64,192]{1,0:T(8,128)(2,1)S(1)} %get-tuple-element.15.xb_ref, ...), custom_call_target="tpu_custom_call" | custom-call | tf_op jit(solution)/shard_map/filter/pallas_call | solution.py:504
Async XLA Ops:
  0.0 0.8 %copy-start = (f32[64,64]{1,0:T(8,128)S(1)}, f32[64,64]{1,0:T(8,128)}, u32[]{:S(2)}) copy-start(f32[64,64]{1,0:T(8,128)} %kernel_hbm.1) | copy-start | bytes 49156
  0.8 0.7 %copy-start.1 = (f32[4096]{0:T(1024)S(1)}, f32[4096]{0:T(1024)}, u32[]{:S(2)}) copy-start(f32[4096]{0:T(1024)} %param.11) | copy-start | bytes 49156
  1.5 0.7 copy-start.2
  2.1 0.7 copy-start.3
  2.8 0.7 copy-start.4
  3.4 0.7 copy-start.5

commit v2 on v1

--- a/solution.py
+++ b/solution.py
@@ -497,7 +497,10 @@
         ] + [each_part] * 6,
         compiler_params=params(collective_id=0),
         name="exchange",
-    )(support_functions, region_shift, owner_counts, kernel, external.reshape(rows_per, LANES), kinetic_taps, magic_taps)
+    )(*(pltpu.with_memory_space_constraint(x, pltpu.HBM) for x in (
+        support_functions, region_shift, owner_counts, kernel, external.reshape(rows_per, LANES),
+        kinetic_taps, magic_taps,
+    )))
 
     slabs = cells // SLAB
     tile = (slabs, local * nx, SLAB)

time: 70.7 us -> 66.4 us (0.939)
  local copies, waits for them, and re-layouts: 4.09 us -> 0.01 us
    unnamed x12 -> x2, local copies, waits for them, and re-layouts: 4.09 us -> 0.01 us
where the time goes in v2:
time: 66.4 us; the launch traced here: 66.3 us
  Pallas kernels  66.3 us (100%)
    pallas_call x1, Pallas kernels, body(): pl.pallas_call(functools.partial(exchange_kernel, devices, parts), out_sh...  58.1 us
    pallas_call x1, Pallas kernels, body(): pl.pallas_call(functools.partial(filter_kernel, devices, rows_per, parts)...  8.18 us

profile of v2, /device:TPU:0, one launch (start us, length us, event | category | flops | bytes accessed | tf_op | source)
XLA Modules:
  0.0 66.3 jit_solution(4065841526630199880)
XLA Ops:
  0.0 0.0 copy-start
  0.0 58.1 %exchange.1 = (bf16[128,192]{1,0:T(8,128)(2,1)S(1)}, bf16[64,192]{1,0:T(8,128)(2,1)S(1)}, bf16[2560,256]{1,0:T(8,128)(2,1)S(1)}, bf16[1536,256]{1,0:T(8,128)(2,1...) custom-call(f32[3,64,2048]{2,1,0:T(8,128)} %slots_hbm.1, s32[3]{0:T(128)} %shift_hbm.1, ...), custom_call_target="tpu_custom_call" | custom-call | tf_op jit(solution)/shard_map/exchange/pallas_call | solution.py:475
  58.1 0.0 copy-done
  58.1 8.2 %filter.1 = f32[2,64,2048]{2,1,0:T(8,128)} custom-call(f32[15]{0:T(128)S(1)} %copy-done, f32[2048,128]{1,0:T(8,128)S(1)} %get-tuple-element.12.got_ref, f32[1280,128]{1,0:T(8,128)S(1)} %bitcast.2, bf16[128,192]{1,0:T(8,128)(2,1)S(1)} %get-tuple-element.14.xf_ref, bf16[64,192]{1,0:T(8,128)(2,1)S(1)} %get-tuple-element.15.xb_ref, ...), custom_call_target="tpu_custom_call" | custom-call | tf_op jit(solution)/shard_map/filter/pallas_call | solution.py:507
Async XLA Ops:
  0.0 58.1 %copy-start = (f32[15]{0:T(128)S(1)}, f32[15]{0:T(128)}, u32[]{:S(2)}) copy-start(f32[15]{0:T(128)} %kin_ref.1) | copy-start | bytes 184

commit v3 on v2

--- a/solution.py
+++ b/solution.py
@@ -40,7 +40,7 @@
     return lax.rem(row, devices) * spread + row // devices
 
 
-def matrices(devices, kin_ref, mag_ref, xf_ref, xb_ref, kin_out, fwd_out, bwd_out):
+def matrices(devices, kin_ref, mag_ref, kx_out, kin_out, fwd_out, xf_ref, xb_ref, bwd_out):
     nx = xb_ref.shape[0]
     kin_half = kin_ref.shape[0]
     taps = mag_ref.shape[0]
@@ -59,17 +59,21 @@
     def iota(shape, dim):
         return lax.broadcasted_iota(jnp.int32, shape, dim)
 
-    spread = max(nx // devices, 1)
-    out_x, in_x = (x_of(iota((nx, nx), d), devices, spread) for d in (0, 1))
+    parts = kx_out.shape[0]
+    plain = iota((nx, nx), 0)
+    out_x, in_x = (x_of(iota((nx, nx), d), devices, parts) for d in (0, 1))
     ahead = lax.rem(in_x - out_x + mag_center + nx, nx)
-    behind = lax.rem(out_x - in_x + mag_center + nx, nx)
-    across = lax.rem(in_x - out_x + kin_center + nx, nx)
+    behind = lax.rem(plain - in_x + mag_center + nx, nx)
+    across = lax.rem(in_x - plain + kin_center + nx, nx)
     fh, fl = halves(picked(ahead, mag) / total)
     kh, kl = halves(picked(across, kin))
     bh, bl = halves(picked(behind, mag) / total)
-    xf_ref[:nx] = jnp.concatenate([fh, fl, fh], axis=1)
-    xf_ref[nx:] = jnp.concatenate([kh, kl, kh], axis=1)
+    xf_ref[...] = jnp.concatenate([fh, fl, fh], axis=1)
     xb_ref[...] = jnp.concatenate([bh, bl, bh], axis=1)
+    each = nx // parts
+    for part in range(parts):
+        columns = slice(part * each, (part + 1) * each)
+        kx_out[part] = jnp.concatenate([kh[:, columns], kl[:, columns], kh[:, columns]], axis=1)
 
     square = (SLAB, SLAB)
     row, col = iota(square, 0), iota(square, 1)
@@ -162,10 +166,23 @@
     return guess - (guess - x / (guess * guess)) * (1.0 / 3.0)
 
 
+def banded(matrix_ref, high, low, slabs, wanted):
+    width = matrix_ref.shape[0] // 2
+    count = width // SLAB
+
+    def wide(at):
+        return jnp.concatenate([
+            jnp.concatenate([at((h + n - count // 2) % slabs) for n in range(count)], axis=1) for h in wanted
+        ], axis=0)
+
+    high, low = wide(high), wide(low)
+    return dot(high, matrix_ref[:width]) + (dot(low, matrix_ref[:width]) + dot(high, matrix_ref[width:]))
+
+
 def exchange_kernel(devices, parts,
                     slots_hbm, shift_hbm, counts_hbm, kernel_hbm, external_hbm, kin_hbm, mag_hbm,
-                    xf_ref, xb_ref, kin_out, fwd_out, bwd_out, back_ref, gpot_ref,
-                    raw_ref, own_ref, out_ref, in_ref, got_ref, mixed_ref, pots_ref,
+                    xf_ref, xb_ref, bwd_out, u_hi, u_lo, acc_ref, gpot_ref,
+                    kx_ref, kin_out, fwd_out, v_hi, v_lo, back_ref, raw_ref, own_ref, out_ref, in_ref, got_ref, mixed_ref, pots_ref,
                     mix_ref, kernel_ref, external_ref, up_ref, down_ref,
                     shift_ref, counts_ref, kin_ref, mag_ref,
                     load_sem, swap_sem, lead_send, lead_recv, part_send, part_recv,
@@ -273,7 +290,55 @@
         got_ref[pl.ds(block(part, me), local * rows), :] = own_ref[pl.ds(block(part, me), local * rows), :]
 
     mixing_matrix(devices, counts_ref, kernel_ref, mix_ref)
-    matrices(devices, kin_ref, mag_ref, xf_ref, xb_ref, kin_out, fwd_out, bwd_out)
+    matrices(devices, kin_ref, mag_ref, kx_ref, kin_out, fwd_out, xf_ref, xb_ref, bwd_out)
+    acc_ref[...] = jnp.zeros_like(acc_ref)
+    slabs = cells // SLAB
+    per_slab = SLAB // LANES
+    each = nx // parts
+    split = max(q_count // rows, 1)
+
+    def forward(part, first, n):
+        group = max(1, min(slabs, GROUP * each // n))
+        length = n * split * local * rows
+        begin = pl.multiple_of((part * devices + first * split) * local * rows, 8)
+        view = back_ref.at[pl.ds(begin, length)]
+
+        def where(f):
+            return pl.ds(pl.multiple_of((part * local + f) * each + first, 16), n)
+
+        for h in range(slabs):
+            for f in range(local):
+                value = jnp.concatenate([
+                    view[pl.ds((q // rows * local + f) * rows + q % rows, n, stride=split * local * rows), :]
+                    for q in range(h * per_slab, (h + 1) * per_slab)
+                ], axis=1)
+                v_hi[h, where(f)], v_lo[h, where(f)] = halves(value)
+
+        def at(ref):
+            return lambda h: jnp.concatenate([ref[h, where(f)] for f in range(local)], axis=0)
+
+        for step in range(0, slabs, group):
+            wanted = range(step, step + group)
+            kinetic = banded(kin_out, at(v_hi), at(v_lo), slabs, wanted)
+            smooth = banded(fwd_out, at(v_hi), at(v_lo), slabs, wanted)
+            for g, h in enumerate(wanted):
+                for f in range(local):
+                    base = (g * local + f) * n
+                    u_hi[h, where(f)], u_lo[h, where(f)] = halves(smooth[base:base + n])
+                    rows_at = pl.ds(pl.multiple_of(f * nx + first * parts, 8), n * parts)
+                    for k in range(per_slab):
+                        target = acc_ref.at[h * per_slab + k, rows_at]
+                        some = pl.ds(part, n, stride=parts) if parts > 1 else slice(None)
+                        target[some, :] += kinetic[base:base + n, k * LANES:(k + 1) * LANES]
+
+    def along_x(part):
+        for h in range(slabs):
+            for f in range(local):
+                here = slice((part * local + f) * each, (part * local + f + 1) * each)
+                high, low = v_hi[h, here], v_lo[h, here]
+                moved = dot(kx_ref[part], jnp.concatenate([high, high, low], axis=0))
+                for k in range(per_slab):
+                    acc_ref[h * per_slab + k, f * nx:(f + 1) * nx, :] += moved[:, k * LANES:(k + 1) * LANES]
 
     def mix(part):
         base = part * functions * rows
@@ -308,7 +373,7 @@
         return peak
 
     peak = None
-    returns, handed, waits = [], [], []
+    returns, waits = [[] for _ in range(parts)], []
     for part in range(parts):
         for copy in arrivals[part]:
             copy.wait_recv()
@@ -336,90 +401,48 @@
                           back_ref.at[pl.ds(block(part, me), local * rows)],
                           back_send.at[part, k], back_recv.at[part, k], there)
             copy.start()
-            returns.append(copy)
+            returns[part].append((k, copy))
         back_ref[pl.ds(block(part, me), local * rows), :] = mixed_ref[pl.ds(block(part, me), local * rows), :]
         gpot_ref[me, begin:begin + extent] = pots_ref[side, begin:begin + extent]
         handed.wait_recv()
         for k in range(1, half):
             waits.append(show(gpot_ref.at[across, span], across, half + k, partner(me, k)))
-    for copy in returns + waits:
+
+    for part in range(parts - 1):
+        for _, copy in returns[part]:
+            copy.wait_recv()
+        forward(part, 0, each)
+        along_x(part)
+    final = parts - 1
+    for near in (True, False):
+        for k, copy in returns[final]:
+            if (k < half) == near:
+                copy.wait_recv()
+        forward(final, (side if near else 1 - side) * (each // 2), each // 2)
+    along_x(final)
+    for copy in waits:
         copy.wait_recv()
-    for copy in [swap, *sends, *returns, *waits]:
+    for copy in [swap, *sends, *waits, *(copy for part in returns for _, copy in part)]:
         copy.wait_send()
 
 
-def filter_kernel(devices, rows_per, parts, kin_ref, got_ref, gpot_ref, xf_ref, xb_ref, kinm_ref, fwd_ref, bwd_ref, out_ref,
-                  v_hi, v_lo, p_hi, p_lo, w_hi, w_lo, acc_ref, pot_ref, stage_ref):
+def filter_kernel(devices, rows_per, kin_ref, u_hi, u_lo, acc_ref, gpot_ref, xf_ref, xb_ref, bwd_ref, out_hbm,
+                  w_hi, w_lo, out_ref, out_sem):
     local, nx, cells = out_ref.shape
     slabs = cells // SLAB
     q_count = cells // LANES
     per_slab = SLAB // LANES
-    spread = max(rows_per // q_count, 1)
-
-    rows = rows_per // parts
+    parts = max(rows_per // q_count, 1)
+    each = nx // parts
     pot_rows = gpot_ref.shape[0] // devices
 
-    def plane(field, q):
-        if field == local:
-            ref, stride, extent = gpot_ref, pot_rows, rows_per
-        else:
-            ref, stride, extent = got_ref, local * rows, rows
-
-        def start(x):
-            if field == local:
-                return x
-            return (x // rows * devices * local + field) * rows + x % rows
-
+    def plane(q):
         if rows_per >= q_count:
             return jnp.concatenate([
-                ref[pl.ds(start(xo * q_count + q), devices, stride=stride), :] for xo in range(spread)
+                gpot_ref[pl.ds(xo * q_count + q, devices, stride=pot_rows), :] for xo in range(parts)
             ], axis=0)
-        split = q_count // extent
-        return ref[pl.ds((q // extent) * stride + start(q % extent), nx, stride=split * stride), :]
-
-    def slab_of(field, h):
-        return jnp.concatenate([plane(field, h * per_slab + k) for k in range(per_slab)], axis=1)
-
-    for h in range(slabs):
-        pot_ref[h] = slab_of(local, h)
-        for f in range(local):
-            high, low = halves(slab_of(f, h))
-            where = slice(f * nx, (f + 1) * nx)
-            v_hi[h, where] = high
-            v_lo[h, where] = low
-            both = dot(xf_ref[...], jnp.concatenate([high, high, low], axis=0))
-            p_hi[h, where], p_lo[h, where] = halves(both[:nx])
-            acc_ref[h, where] = both[nx:]
-
-    def banded(hi_ref, lo_ref, matrix_ref, h):
-        width = matrix_ref.shape[0] // 2
-        count = width // SLAB
-
-        def wide(ref):
-            return jnp.concatenate([
-                jnp.concatenate(
-                    [ref[lax.rem(h + g + (n - count // 2) + slabs, slabs)] for n in range(count)], axis=1
-                ) for g in range(GROUP)
-            ], axis=0)
-
-        high, low = wide(hi_ref), wide(lo_ref)
-        return dot(high, matrix_ref[:width]) + (dot(low, matrix_ref[:width]) + dot(high, matrix_ref[width:]))
-
-    def forward(step, carry):
-        h = step * GROUP
-        kinetic = banded(v_hi, v_lo, kinm_ref, h)
-        smooth = banded(p_hi, p_lo, fwd_ref, h)
-        for g in range(GROUP):
-            base = g * local * nx
-            acc_ref[h + g] += kinetic[base:base + local * nx]
-            potential = pot_ref[h + g]
-            for f in range(local):
-                high, low = halves(smooth[base + f * nx:base + (f + 1) * nx] * potential)
-                mixed = dot(xb_ref[...], jnp.concatenate([high, high, low], axis=0))
-                w_hi[h + g, f * nx:(f + 1) * nx], w_lo[h + g, f * nx:(f + 1) * nx] = halves(mixed)
-        return carry
-
-    lax.fori_loop(0, slabs // GROUP, forward, 0)
+        split = q_count // rows_per
+        return gpot_ref[pl.ds((q // rows_per) * pot_rows + q % rows_per, nx, stride=split * pot_rows), :]
 
     sides = jnp.abs(kin_ref[0])
     for t in range(1, kin_ref.shape[0]):
@@ -428,28 +451,36 @@
     for e in range(1, devices):
         peaks = jnp.maximum(peaks, gpot_ref[e * pot_rows + rows_per:(e + 1) * pot_rows, :])
     bound = 1.0 + 1.5 * sides + jnp.max(peaks)
-
-    def backward(step, carry):
-        first = step * GROUP
-        back = banded(w_hi, w_lo, bwd_ref, first)
-        count = nx // spread
-        for g in range(GROUP):
-            h = first + g
-            result = (acc_ref[h] + back[g * local * nx:(g + 1) * local * nx]) / bound
+    scale = 1.0 / jnp.full((1, SLAB), bound, F32)
+
+    for h in range(slabs):
+        potential = jnp.concatenate([plane(h * per_slab + k) for k in range(per_slab)], axis=1)
+        for f in range(local):
+            def taken(ref):
+                starts = [(part * local + f) * each for part in range(parts)]
+                return jnp.concatenate([ref[h, start:start + each] for start in starts], axis=0)
+
+            high, low = taken(u_hi), taken(u_lo)
+            smooth = dot(xf_ref[...], jnp.concatenate([high, high, low], axis=0))
+            high, low = halves(smooth * potential)
+            moved = dot(xb_ref[...], jnp.concatenate([high, high, low], axis=0))
+            w_hi[h, f * nx:(f + 1) * nx], w_lo[h, f * nx:(f + 1) * nx] = halves(moved)
+
+    copies = []
+    for step in range(0, slabs, GROUP):
+        wanted = range(step, step + GROUP)
+        back = banded(bwd_ref, lambda h: w_hi[h], lambda h: w_lo[h], slabs, wanted)
+        for g, h in enumerate(wanted):
+            kinetic = jnp.concatenate([acc_ref[h * per_slab + k] for k in range(per_slab)], axis=1)
+            result = (kinetic + back[g * local * nx:(g + 1) * local * nx]) * scale
             for f in range(local):
-                for k in range(per_slab):
-                    q = h * per_slab + k
-                    if spread > 1:
-                        for xo in range(spread):
-                            block = result[f * nx + xo * count:f * nx + (xo + 1) * count, k * LANES:(k + 1) * LANES]
-                            stage_ref[f, q, pl.ds(xo, count, stride=spread), :] = block
-                        ordered = stage_ref[f, q]
-                    else:
-                        ordered = result[f * nx:(f + 1) * nx, k * LANES:(k + 1) * LANES]
-                    out_ref[f, :, pl.ds(pl.multiple_of(q * LANES, LANES), LANES)] = ordered
-        return carry
-
-    lax.fori_loop(0, slabs // GROUP, backward, 0)
+                out_ref[f, :, h * SLAB:(h + 1) * SLAB] = result[f * nx:(f + 1) * nx]
+        columns = pl.ds(step * SLAB, GROUP * SLAB)
+        copy = pltpu.make_async_copy(out_ref.at[:, :, columns], out_hbm.at[:, :, columns], out_sem.at[len(copies)])
+        copy.start()
+        copies.append(copy)
+    for copy in copies:
+        copy.wait()
 
 
 def shaped(shape, dtype=F32):
@@ -463,7 +494,7 @@
     local = functions // devices
     rows_per = nx * cells // devices // LANES
     q_count = cells // LANES
-    parts = 2 if rows_per % (2 * q_count) == 0 else 1
+    parts = max(rows_per // q_count, 1)
     rows = rows_per // parts
     reach = -(-(magic_taps.shape[0] // 2) // YS)
     kin_reach = -(-(kinetic_taps.shape[0] - 1) // YS)
@@ -472,20 +503,26 @@
     each_part = pltpu.SemaphoreType.DMA((parts, devices))
     flat = (nx * q_count, LANES)
     whole = (functions * rows_per, LANES)
-    xf, xb, kin_m, fwd_m, bwd_m, back, gpot = pl.pallas_call(
+    slabs = cells // SLAB
+    tile = (slabs, local * nx, SLAB)
+    kin_band = pltpu.VMEM((2 * (2 * kin_reach + 1) * SLAB, SLAB), BF16)
+    mag_band = (2 * (2 * reach + 1) * SLAB, SLAB)
+    xf, xb, bwd_m, u_hi, u_lo, acc, gpot = pl.pallas_call(
         functools.partial(exchange_kernel, devices, parts),
         out_shape=(
-            shaped((2 * nx, 3 * nx), BF16),
             shaped((nx, 3 * nx), BF16),
-            shaped((2 * (2 * kin_reach + 1) * SLAB, SLAB), BF16),
-            shaped((2 * (2 * reach + 1) * SLAB, SLAB), BF16),
-            shaped((2 * (2 * reach + 1) * SLAB, SLAB), BF16),
-            shaped(whole),
+            shaped((nx, 3 * nx), BF16),
+            shaped(mag_band, BF16),
+            shaped(tile, BF16),
+            shaped(tile, BF16),
+            shaped((q_count, local * nx, LANES)),
             shaped((devices, rows_per + 8, LANES)),
         ),
         in_specs=[HBM] * 7,
         out_specs=(VMEM,) * 7,
         scratch_shapes=[
+            pltpu.VMEM((parts, nx, 3 * nx // parts), BF16), kin_band, pltpu.VMEM(mag_band, BF16),
+            pltpu.VMEM(tile, BF16), pltpu.VMEM(tile, BF16), pltpu.VMEM(whole, F32),
             pltpu.VMEM((slot_each, nx, cells), F32), pltpu.VMEM(whole, F32),
             pltpu.VMEM(flat, F32), pltpu.VMEM(flat, F32), pltpu.VMEM(whole, F32), pltpu.VMEM(whole, F32),
             pltpu.VMEM((2, rows_per + 8, LANES), F32), pltpu.VMEM((functions, 3 * functions), BF16),
@@ -502,19 +539,18 @@
         kinetic_taps, magic_taps,
     )))
 
-    slabs = cells // SLAB
-    tile = (slabs, local * nx, SLAB)
     return pl.pallas_call(
-        functools.partial(filter_kernel, devices, rows_per, parts),
+        functools.partial(filter_kernel, devices, rows_per),
         out_shape=shaped((local, nx, cells)),
         in_specs=[SMEM] + [VMEM] * 7,
-        out_specs=VMEM,
-        scratch_shapes=[pltpu.VMEM(tile, BF16)] * 6
-        + [pltpu.VMEM(tile, F32), pltpu.VMEM((slabs, nx, SLAB), F32),
-           pltpu.VMEM((local, cells // LANES, nx, LANES), F32)],
+        out_specs=HBM,
+        scratch_shapes=[
+            pltpu.VMEM(tile, BF16), pltpu.VMEM(tile, BF16), pltpu.VMEM((local, nx, cells), F32),
+            pltpu.SemaphoreType.DMA((slabs // GROUP,)),
+        ],
         compiler_params=params(),
         name="filter",
-    )(kinetic_taps, back, gpot.reshape(-1, LANES), xf, xb, kin_m, fwd_m, bwd_m)
+    )(kinetic_taps, u_hi, u_lo, acc, gpot.reshape(-1, LANES), xf, xb, bwd_m)
 
 
 def solution(mesh):

time: 66.4 us -> 63.2 us (0.952); the launches traced: 66.3 us -> 62.4 us
  Pallas kernels: 66.3 us -> 62.2 us
    pallas_call x1, Pallas kernels: 8.18 us -> 3.64 us  [body(): pl.pallas_call(functools.partial(filter_kernel, devices, rows_per), out_s...]
where the time goes in v3:
time: 63.2 us; the launch traced here: 62.4 us
  Pallas kernels  62.2 us (98%)
    pallas_call x1, Pallas kernels, body(): pl.pallas_call(functools.partial(exchange_kernel, devices, parts), out_sh...  58.6 us
    pallas_call x1, Pallas kernels, body(): pl.pallas_call(functools.partial(filter_kernel, devices, rows_per), out_s...  3.64 us

profile of v3, /device:TPU:0, one launch (start us, length us, event | category | flops | bytes accessed | tf_op | source)
XLA Modules:
  0.0 62.4 jit_solution(4854812382262605881)
XLA Ops:
  0.0 0.0 copy-start
  0.0 58.6 %exchange.1 = (bf16[64,192]{1,0:T(8,128)(2,1)S(1)}, bf16[64,192]{1,0:T(8,128)(2,1)S(1)}, bf16[1536,256]{1,0:T(8,128)(2,1)S(1)}, bf16[8,128,256]{2,1,0:T(8,128)(2...) custom-call(f32[3,64,2048]{2,1,0:T(8,128)} %slots_hbm.1, ...), custom_call_target="tpu_custom_call" | custom-call | tf_op jit(solution)/shard_map/exchange/pallas_call | solution.py:510
  58.6 0.0 copy-done
  58.6 3.6 %filter.1 = f32[2,64,2048]{2,1,0:T(8,128)} custom-call(f32[15]{0:T(128)S(1)} %copy-done, bf16[8,128,256]{2,1,0:T(8,128)(2,1)S(1)} %get-tuple-element.12.u_hi, bf16[8,128,256]{2,1,0:T(8,128)(2,1)S(1)} %get-tuple-element.13.u_lo, f32[16,128,128]{2,1,0:T(8,128)S(1)} %get-tuple-element.14.acc_ref, f32[1280,128]{1,0:T(8,128)S(1)} %bitcast.2, ...), custom_call_target="tpu_custom_call" | custom-call | tf_op jit(solution)/shard_map/filter/pallas_call | solution.py:542
Async XLA Ops:
  0.0 58.6 %copy-start = (f32[15]{0:T(128)S(1)}, f32[15]{0:T(128)}, u32[]{:S(2)}) copy-start(f32[15]{0:T(128)} %kin_ref.1) | copy-start | bytes 184

commit v4 on v3

--- a/solution.py
+++ b/solution.py
@@ -14,7 +14,6 @@
 YS = SLAB // NZ
 GROUP = 4
 VMEM = pl.BlockSpec(memory_space=pltpu.VMEM)
-SMEM = pl.BlockSpec(memory_space=pltpu.SMEM)
 HBM = pl.BlockSpec(memory_space=pltpu.HBM)
 F32 = jnp.float32
 BF16 = jnp.bfloat16
@@ -181,7 +180,7 @@
 
 def exchange_kernel(devices, parts,
                     slots_hbm, shift_hbm, counts_hbm, kernel_hbm, external_hbm, kin_hbm, mag_hbm,
-                    xf_ref, xb_ref, bwd_out, u_hi, u_lo, acc_ref, gpot_ref,
+                    xf_ref, xb_ref, bwd_out, u_hi, u_lo, acc_ref, sides_ref, gpot_ref,
                     kx_ref, kin_out, fwd_out, v_hi, v_lo, back_ref, raw_ref, own_ref, out_ref, in_ref, got_ref, mixed_ref, pots_ref,
                     mix_ref, kernel_ref, external_ref, up_ref, down_ref,
                     shift_ref, counts_ref, kin_ref, mag_ref,
@@ -292,13 +291,17 @@
     mixing_matrix(devices, counts_ref, kernel_ref, mix_ref)
     matrices(devices, kin_ref, mag_ref, kx_ref, kin_out, fwd_out, xf_ref, xb_ref, bwd_out)
     acc_ref[...] = jnp.zeros_like(acc_ref)
+    sides = jnp.abs(kin_ref[0])
+    for t in range(1, kin_ref.shape[0]):
+        sides = sides + 2.0 * jnp.abs(kin_ref[t])
+    sides_ref[...] = jnp.full(sides_ref.shape, 1.0 + 1.5 * sides, F32)
     slabs = cells // SLAB
     per_slab = SLAB // LANES
     each = nx // parts
     split = max(q_count // rows, 1)
 
     def forward(part, first, n):
-        group = max(1, min(slabs, GROUP * each // n))
+        group = GROUP
         length = n * split * local * rows
         begin = pl.multiple_of((part * devices + first * split) * local * rows, 8)
         view = back_ref.at[pl.ds(begin, length)]
@@ -381,9 +384,9 @@
         peak = here if peak is None else jnp.maximum(peak, here)
         begin, extent = part * rows, rows
         if part == parts - 1:
-            extent = rows + 8
+            extent = rows + 1
             for spin in range(2):
-                pots_ref[spin, rows_per:] = peak
+                pots_ref[spin, rows_per:rows_per + 1] = jnp.max(peak, axis=0, keepdims=True)
         span = pl.ds(begin, extent)
 
         def show(source, owner, slot, there):
@@ -426,7 +429,7 @@
         copy.wait_send()
 
 
-def filter_kernel(devices, rows_per, kin_ref, u_hi, u_lo, acc_ref, gpot_ref, xf_ref, xb_ref, bwd_ref, out_hbm,
+def filter_kernel(devices, rows_per, u_hi, u_lo, acc_ref, sides_ref, gpot_ref, xf_ref, xb_ref, bwd_ref, out_hbm,
                   w_hi, w_lo, out_ref, out_sem):
     local, nx, cells = out_ref.shape
     slabs = cells // SLAB
@@ -444,14 +447,9 @@
         split = q_count // rows_per
         return gpot_ref[pl.ds((q // rows_per) * pot_rows + q % rows_per, nx, stride=split * pot_rows), :]
 
-    sides = jnp.abs(kin_ref[0])
-    for t in range(1, kin_ref.shape[0]):
-        sides = sides + 2.0 * jnp.abs(kin_ref[t])
-    peaks = gpot_ref[rows_per:pot_rows, :]
-    for e in range(1, devices):
-        peaks = jnp.maximum(peaks, gpot_ref[e * pot_rows + rows_per:(e + 1) * pot_rows, :])
-    bound = 1.0 + 1.5 * sides + jnp.max(peaks)
-    scale = 1.0 / jnp.full((1, SLAB), bound, F32)
+    peaks = gpot_ref[pl.ds(rows_per, devices, stride=pot_rows), :]
+    bound = sides_ref[:1, :] + jnp.max(peaks)
+    scale = jnp.concatenate([1.0 / bound] * per_slab, axis=1)
 
     for h in range(slabs):
         potential = jnp.concatenate([plane(h * per_slab + k) for k in range(per_slab)], axis=1)
@@ -467,15 +465,16 @@
             w_hi[h, f * nx:(f + 1) * nx], w_lo[h, f * nx:(f + 1) * nx] = halves(moved)
 
     copies = []
-    for step in range(0, slabs, GROUP):
-        wanted = range(step, step + GROUP)
+    group = slabs // out_sem.shape[0]
+    for step in range(0, slabs, group):
+        wanted = range(step, step + group)
         back = banded(bwd_ref, lambda h: w_hi[h], lambda h: w_lo[h], slabs, wanted)
         for g, h in enumerate(wanted):
             kinetic = jnp.concatenate([acc_ref[h * per_slab + k] for k in range(per_slab)], axis=1)
             result = (kinetic + back[g * local * nx:(g + 1) * local * nx]) * scale
             for f in range(local):
                 out_ref[f, :, h * SLAB:(h + 1) * SLAB] = result[f * nx:(f + 1) * nx]
-        columns = pl.ds(step * SLAB, GROUP * SLAB)
+        columns = pl.ds(step * SLAB, group * SLAB)
         copy = pltpu.make_async_copy(out_ref.at[:, :, columns], out_hbm.at[:, :, columns], out_sem.at[len(copies)])
         copy.start()
         copies.append(copy)
@@ -507,7 +506,7 @@
     tile = (slabs, local * nx, SLAB)
     kin_band = pltpu.VMEM((2 * (2 * kin_reach + 1) * SLAB, SLAB), BF16)
     mag_band = (2 * (2 * reach + 1) * SLAB, SLAB)
-    xf, xb, bwd_m, u_hi, u_lo, acc, gpot = pl.pallas_call(
+    xf, xb, bwd_m, u_hi, u_lo, acc, sides, gpot = pl.pallas_call(
         functools.partial(exchange_kernel, devices, parts),
         out_shape=(
             shaped((nx, 3 * nx), BF16),
@@ -516,10 +515,11 @@
             shaped(tile, BF16),
             shaped(tile, BF16),
             shaped((q_count, local * nx, LANES)),
+            shaped((8, LANES)),
             shaped((devices, rows_per + 8, LANES)),
         ),
         in_specs=[HBM] * 7,
-        out_specs=(VMEM,) * 7,
+        out_specs=(VMEM,) * 8,
         scratch_shapes=[
             pltpu.VMEM((parts, nx, 3 * nx // parts), BF16), kin_band, pltpu.VMEM(mag_band, BF16),
             pltpu.VMEM(tile, BF16), pltpu.VMEM(tile, BF16), pltpu.VMEM(whole, F32),
@@ -542,15 +542,15 @@
     return pl.pallas_call(
         functools.partial(filter_kernel, devices, rows_per),
         out_shape=shaped((local, nx, cells)),
-        in_specs=[SMEM] + [VMEM] * 7,
+        in_specs=[VMEM] * 8,
         out_specs=HBM,
         scratch_shapes=[
             pltpu.VMEM(tile, BF16), pltpu.VMEM(tile, BF16), pltpu.VMEM((local, nx, cells), F32),
-            pltpu.SemaphoreType.DMA((slabs // GROUP,)),
+            pltpu.SemaphoreType.DMA((4,)),
         ],
         compiler_params=params(),
         name="filter",
-    )(kinetic_taps, u_hi, u_lo, acc, gpot.reshape(-1, LANES), xf, xb, bwd_m)
+    )(u_hi, u_lo, acc, sides, gpot.reshape(-1, LANES), xf, xb, bwd_m)
 
 
 def solution(mesh):

time: 63.2 us -> 61 us (0.965)
  Pallas kernels: 62.2 us -> 60.4 us
    pallas_call x1, Pallas kernels: 58.6 us -> 57.4 us  [body(): pl.pallas_call(functools.partial(exchange_kernel, devices, parts), out_sh...]
    pallas_call x1, Pallas kernels: 3.64 us -> 2.94 us  [body(): pl.pallas_call(functools.partial(filter_kernel, devices, rows_per), out_s...]
where the time goes in v4:
time: 61 us; the launch traced here: 60.5 us
  Pallas kernels  60.4 us (99%)
    pallas_call x1, Pallas kernels, body(): pl.pallas_call(functools.partial(exchange_kernel, devices, parts), out_sh...  57.4 us
    pallas_call x1, Pallas kernels, body(): pl.pallas_call(functools.partial(filter_kernel, devices, rows_per), out_s...  2.94 us

profile of v4, /device:TPU:0, one launch (start us, length us, event | category | flops | bytes accessed | tf_op | source)
XLA Modules:
  0.0 60.5 jit_solution(10557121149148116952)
XLA Ops:
  0.0 57.4 %exchange.1 = (bf16[64,192]{1,0:T(8,128)(2,1)S(1)}, bf16[64,192]{1,0:T(8,128)(2,1)S(1)}, bf16[1536,256]{1,0:T(8,128)(2,1)S(1)}, bf16[8,128,256]{2,1,0:T(8,128)(2...) custom-call(f32[3,64,2048]{2,1,0:T(8,128)} %slots_hbm.1, ...), custom_call_target="tpu_custom_call" | custom-call | tf_op jit(solution)/shard_map/exchange/pallas_call | solution.py:509
  57.4 2.9 %filter.1 = f32[2,64,2048]{2,1,0:T(8,128)} custom-call(bf16[8,128,256]{2,1,0:T(8,128)(2,1)S(1)} %get-tuple-element.13.u_hi, bf16[8,128,256]{2,1,0:T(8,128)(2,1)S(1)} %get-tuple-element.14.u_lo, f32[16,128,128]{2,1,0:T(8,128)S(1)} %get-tuple-element.15.acc_ref, f32[8,128]{1,0:T(8,128)S(1)} %get-tuple-element.16.sides_ref, f32[1280,128]{1,0:T(8,128)S(1)} %bitcast.2, ...), custom_call_target="tpu_custom_call" | custom-call | tf_op jit(solution)/shard_map/filter/pallas_call | solution.py:542

commit v5 on v4

--- a/solution.py
+++ b/solution.py
@@ -208,11 +208,6 @@
     shift_load = load(shift_hbm, shift_ref, slot_each)
     for s in reversed(range(1, slot_each)):
         slot_loads[s] = load(slots_hbm.at[s], raw_ref.at[s], s)
-    small = [load(a, b, slot_each + 1 + k) for k, (a, b) in enumerate((
-        (counts_hbm, counts_ref), (kernel_hbm, kernel_ref), (external_hbm, external_ref),
-        (kin_hbm, kin_ref), (mag_hbm, mag_ref),
-    ))]
-
     barrier = pltpu.get_barrier_semaphore()
     for k in range(1, devices):
         pl.semaphore_signal(barrier, inc=1, device_id=(partner(me, k),), device_id_type=pl.DeviceIdType.MESH)
@@ -266,6 +261,10 @@
     for k in order:
         give(0, 0, 1, k, lead_send, lead_recv)
     last = slot_each - 1
+    small = [load(a, b, slot_each + 1 + k) for k, (a, b) in enumerate((
+        (counts_hbm, counts_ref), (kernel_hbm, kernel_ref), (external_hbm, external_ref),
+        (kin_hbm, kin_ref), (mag_hbm, mag_ref),
+    ))]
     rolled(last, out_ref, 1, 0)
     swap = remote(out_ref, in_ref, swap_sem.at[0], swap_sem.at[1], mate)
     swap.start()
@@ -411,21 +410,28 @@
         for k in range(1, half):
             waits.append(show(gpot_ref.at[across, span], across, half + k, partner(me, k)))
 
+    for copy in [swap, *sends]:
+        copy.wait_send()
     for part in range(parts - 1):
         for _, copy in returns[part]:
             copy.wait_recv()
         forward(part, 0, each)
+        for _, copy in returns[part]:
+            copy.wait_send()
         along_x(part)
     final = parts - 1
+    late = waits[1 - half:]
+    for copy in waits[:1 - half]:
+        copy.wait()
     for near in (True, False):
         for k, copy in returns[final]:
             if (k < half) == near:
                 copy.wait_recv()
         forward(final, (side if near else 1 - side) * (each // 2), each // 2)
     along_x(final)
-    for copy in waits:
+    for copy in late:
         copy.wait_recv()
-    for copy in [swap, *sends, *waits, *(copy for part in returns for _, copy in part)]:
+    for copy in [*late, *(copy for _, copy in returns[final])]:
         copy.wait_send()
 
 

time: 61 us -> 60.7 us (level)
  no operation moved by 1% of the time
where the time goes in v5:
time: 60.7 us; the launch traced here: 60.2 us
  Pallas kernels  60 us (99%)
    pallas_call x1, Pallas kernels, body(): pl.pallas_call(functools.partial(exchange_kernel, devices, parts), out_sh...  57.1 us
    pallas_call x1, Pallas kernels, body(): pl.pallas_call(functools.partial(filter_kernel, devices, rows_per), out_s...  2.94 us

profile of v5, /device:TPU:0, one launch (start us, length us, event | category | flops | bytes accessed | tf_op | source)
XLA Modules:
  0.0 60.2 jit_solution(4083648653043561602)
XLA Ops:
  0.0 57.1 %exchange.1 = (bf16[64,192]{1,0:T(8,128)(2,1)S(1)}, bf16[64,192]{1,0:T(8,128)(2,1)S(1)}, bf16[1536,256]{1,0:T(8,128)(2,1)S(1)}, bf16[8,128,256]{2,1,0:T(8,128)(2...) custom-call(f32[3,64,2048]{2,1,0:T(8,128)} %slots_hbm.1, ...), custom_call_target="tpu_custom_call" | custom-call | tf_op jit(solution)/shard_map/exchange/pallas_call | solution.py:515
  57.1 2.9 %filter.1 = f32[2,64,2048]{2,1,0:T(8,128)} custom-call(bf16[8,128,256]{2,1,0:T(8,128)(2,1)S(1)} %get-tuple-element.13.u_hi, bf16[8,128,256]{2,1,0:T(8,128)(2,1)S(1)} %get-tuple-element.14.u_lo, f32[16,128,128]{2,1,0:T(8,128)S(1)} %get-tuple-element.15.acc_ref, f32[8,128]{1,0:T(8,128)S(1)} %get-tuple-element.16.sides_ref, f32[1280,128]{1,0:T(8,128)S(1)} %bitcast.2, ...), custom_call_target="tpu_custom_call" | custom-call | tf_op jit(solution)/shard_map/filter/pallas_call | solution.py:548

commit v6 on v5

--- a/solution.py
+++ b/solution.py
@@ -471,8 +471,8 @@
             w_hi[h, f * nx:(f + 1) * nx], w_lo[h, f * nx:(f + 1) * nx] = halves(moved)
 
     copies = []
-    group = slabs // out_sem.shape[0]
-    for step in range(0, slabs, group):
+    step = 0
+    for group in [2] * (slabs // 2 - 1) + [1, 1]:
         wanted = range(step, step + group)
         back = banded(bwd_ref, lambda h: w_hi[h], lambda h: w_lo[h], slabs, wanted)
         for g, h in enumerate(wanted):
@@ -484,6 +484,7 @@
         copy = pltpu.make_async_copy(out_ref.at[:, :, columns], out_hbm.at[:, :, columns], out_sem.at[len(copies)])
         copy.start()
         copies.append(copy)
+        step += group
     for copy in copies:
         copy.wait()
 
@@ -552,7 +553,7 @@
         out_specs=HBM,
         scratch_shapes=[
             pltpu.VMEM(tile, BF16), pltpu.VMEM(tile, BF16), pltpu.VMEM((local, nx, cells), F32),
-            pltpu.SemaphoreType.DMA((4,)),
+            pltpu.SemaphoreType.DMA((slabs // 2 + 1,)),
         ],
         compiler_params=params(),
         name="filter",

time: 60.7 us -> 60.7 us (level)
  no operation moved by 1% of the time
where the time goes in v6:
time: 60.7 us; the launch traced here: 60.2 us
  Pallas kernels  60 us (99%)
    pallas_call x1, Pallas kernels, body(): pl.pallas_call(functools.partial(exchange_kernel, devices, parts), out_sh...  57.1 us
    pallas_call x1, Pallas kernels, body(): pl.pallas_call(functools.partial(filter_kernel, devices, rows_per), out_s...  2.95 us

profile of v6, /device:TPU:0, one launch (start us, length us, event | category | flops | bytes accessed | tf_op | source)
XLA Modules:
  0.0 60.2 jit_solution(9998990897097583031)
XLA Ops:
  0.0 57.1 %exchange.1 = (bf16[64,192]{1,0:T(8,128)(2,1)S(1)}, bf16[64,192]{1,0:T(8,128)(2,1)S(1)}, bf16[1536,256]{1,0:T(8,128)(2,1)S(1)}, bf16[8,128,256]{2,1,0:T(8,128)(2...) custom-call(f32[3,64,2048]{2,1,0:T(8,128)} %slots_hbm.1, ...), custom_call_target="tpu_custom_call" | custom-call | tf_op jit(solution)/shard_map/exchange/pallas_call | solution.py:516
  57.1 2.9 %filter.1 = f32[2,64,2048]{2,1,0:T(8,128)} custom-call(bf16[8,128,256]{2,1,0:T(8,128)(2,1)S(1)} %get-tuple-element.13.u_hi, bf16[8,128,256]{2,1,0:T(8,128)(2,1)S(1)} %get-tuple-element.14.u_lo, f32[16,128,128]{2,1,0:T(8,128)S(1)} %get-tuple-element.15.acc_ref, f32[8,128]{1,0:T(8,128)S(1)} %get-tuple-element.16.sides_ref, f32[1280,128]{1,0:T(8,128)S(1)} %bitcast.2, ...), custom_call_target="tpu_custom_call" | custom-call | tf_op jit(solution)/shard_map/filter/pallas_call | solution.py:549
